TPU v7x, 512 devices: a whole 4x4x16 slice. The times are simulated.
512 devices in a mesh: dp: 16 (over z_hi, y), feat: 32 (over x, z_lo, core).
Axes of the slice: x: 4, y: 4, z: 16 (z_hi: 4, z_lo: 4; z = z_hi * 4 + z_lo), core: 2. Of those that a mesh axis runs over, the one named last changes fastest.
Arguments:
- sample: bfloat16 [16384, 2048], P(('dp', 'feat')), may hold values from -1800 to 1800
- pool: bfloat16 [32768, 2048], P(('dp', 'feat')), may hold values from -720 to 720
- old_min: float32 [32768], P(('dp', 'feat')), may hold values from 0.5 to 1.5
- centers: int32 [256], replicated, may hold values from 0 to 32767
Outputs:
- new_min: float32 [32768], P(('dp', 'feat'))
All inputs are finite; a program needn't handle non-finite values.
Results may differ from a plain program's by a relative error of at most 0.00045.
Values may be sent and summed in bfloat16 or wider, within the bound.
A program may use at most 64 MiB of HBM per device.

v0:
```python
import jax
import jax.numpy as jnp
from jax import lax
from jax.sharding import PartitionSpec as P

EPSILON = 1e-06
HIGHEST = lax.Precision.HIGHEST


def contract_rows(left_part, right_part):
    return lax.dot_general(
        left_part, right_part, (((0,), (0,)), ((), ())), preferred_element_type=jnp.float32
    )


def squared_terms(row_values, centre_rows):
    row_wide = row_values.astype(jnp.float32)
    centre_wide = centre_rows.astype(jnp.float32)
    row_norms = jnp.sum(row_wide * row_wide, axis=1)
    centre_norms = jnp.sum(centre_wide * centre_wide, axis=1)
    inner_products = lax.dot_general(
        row_values, centre_rows, (((1,), (1,)), ((), ())), preferred_element_type=jnp.float32
    )
    return row_norms[:, None] + centre_norms[None, :] - 2.0 * inner_products


def pick_rows(source, centers, offset):
    row_count = source.shape[0]
    local_index = centers - offset
    inside = (local_index >= 0) & (local_index < row_count)
    taken_rows = source[jnp.clip(local_index, 0, row_count - 1)].astype(jnp.float32)
    return jnp.where(inside[:, None], taken_rows, 0.0)


def per_device(sample, pool, old_min, centers):
    model_width = sample.shape[1]
    feat_count = lax.axis_size("feat")
    group_count = lax.axis_size("dp")
    row_block = model_width // feat_count
    col_block = model_width // group_count
    feat_index = lax.axis_index("feat")
    group_index = lax.axis_index("dp")
    row_start = feat_index * row_block
    col_start = group_index * col_block
    pool_count = pool.shape[0]
    sample_total = sample.shape[0] * feat_count * group_count
    row_offset = (group_index * feat_count + feat_index) * pool_count
    sample_wide = sample.astype(jnp.float32)
    own_squares = jnp.sum(sample_wide * sample_wide, axis=0)
    col_squares = lax.psum(own_squares, ("dp", "feat"))
    inverse = 1.0 / jnp.sqrt(col_squares / sample_total + EPSILON)
    portion = lax.all_gather(sample, "feat", axis=0, tiled=True)
    left_part = lax.dynamic_slice_in_dim(portion, row_start, row_block, 1)
    gram_part = contract_rows(left_part, portion)
    gram_part = gram_part / sample_total
    inverse_rows = lax.dynamic_slice_in_dim(inverse, row_start, row_block)
    inverse_cols = lax.dynamic_slice_in_dim(inverse, col_start, col_block)
    cov_block = lax.psum_scatter(gram_part, "dp", scatter_dimension=1, tiled=True)
    corr_block = inverse_rows[:, None] * cov_block * inverse_cols[None, :]
    corr_rows = lax.all_gather(corr_block, "dp", axis=1, tiled=True)
    corr_cols = lax.all_gather(corr_block, "feat", axis=0, tiled=True)
    rows_global = row_start + jnp.arange(row_block, dtype=jnp.int32)
    cols_global = col_start + jnp.arange(col_block, dtype=jnp.int32)
    all_index = jnp.arange(model_width, dtype=jnp.int32)
    eye_rows = (rows_global[:, None] == all_index[None, :]).astype(jnp.float32)
    eye_cols = (all_index[:, None] == cols_global[None, :]).astype(jnp.float32)
    eye_block = (rows_global[:, None] == cols_global[None, :]).astype(jnp.float32)
    first_rows = 0.5 * (3.0 * eye_rows - corr_rows)
    first_cols = 0.5 * (3.0 * eye_cols - corr_cols)
    updated_y = jnp.dot(corr_rows, first_cols, precision=HIGHEST)
    left_part = first_rows
    middle = jnp.dot(
        left_part, lax.all_gather(updated_y, "feat", axis=0, tiled=True), precision=HIGHEST
    )
    second_factor = 0.5 * (3.0 * eye_block - middle)
    root_block = jnp.dot(
        lax.all_gather(second_factor, "dp", axis=1, tiled=True), first_cols, precision=HIGHEST
    )
    weight_block = (inverse_rows[:, None] * root_block).astype(jnp.bfloat16)
    weight_cols = lax.all_gather(weight_block, "feat", axis=0, tiled=True)
    everything = jnp.dot(
        pool,
        lax.all_gather(weight_cols, "dp", axis=1, tiled=True),
        preferred_element_type=jnp.float32,
    ).astype(jnp.bfloat16)
    contribution = pick_rows(everything, centers, row_offset)
    centre_full = lax.psum(contribution, ("dp", "feat")).astype(jnp.bfloat16)
    squared = squared_terms(everything, centre_full)
    nearest = jnp.min(jnp.maximum(squared, 0.0), axis=1) / (2.0 * model_width)
    return jnp.minimum(old_min, nearest)


def solution(mesh):
    return jax.shard_map(
        per_device,
        mesh=mesh,
        in_specs=(P(("dp", "feat"), None), P(("dp", "feat"), None), P(("dp", "feat")), P()),
        out_specs=P(("dp", "feat")),
        check_vma=False,
    )
```

profile of v0, /device:TPU:1, one launch (start us, length us, event | category | flops | bytes accessed | tf_op | source)
XLA Modules:
  0.0 781.0 jit_solution(9917778738509852095)
XLA Ops:
  6.5 0.7 all-gather.5.cloned.1.call-update
  7.3 76.0 %all-gather.5.cloned.1.call-done = bf16[1024,2048]{1,0:T(8,128)(2,1)} async-done(((bf16[32,2048]{1,0:T(8,128)(2,1)}), bf16[1024,2048]{1,0:T(8,128)(2,1)}) %all-gather.5.cloned.1.call-update) | async-done | bytes 4194320 | tf_op jit(solution)/shard_map/all_gather | solution.py:52
  83.3 4.0 convolution_multiply_fusion
  87.5 105.5 %psum.14 = f32[2048]{0:T(1024)S(1)} all-reduce(f32[2048]{0:T(1024)S(1)} %multiply_reduce_fusion.2), channel_id=1, replica_groups=mesh['dp'=16,'feat'=32] {'dp','feat'}, use_global_device_ids=true, to_apply=%region_1.0 | all-reduce | flops 2048 | bytes 16384 | tf_op jit(solution)/shard_map/psum | solution.py:50
  193.0 0.1 dynamic_slice.9
  193.1 0.1 dynamic_slice.11
  193.2 3.6 reduce-scatter.2.cloned.1.call-done
  196.7 1.4 multiply_multiply_fusion
  198.2 51.9 %all_gather.22 = f32[64,2048]{1,0:T(8,128)S(1)} all-gather(f32[64,128]{1,0:T(8,128)} %multiply_multiply_fusion), channel_id=1, replica_groups=mesh['dp'=16,'feat'=32] {'dp'}, dimensions={1}, use_global_device_ids=true | all-gather | bytes 557056 | tf_op jit(solution)/shard_map/all_gather | solution.py:60
  250.2 11.2 %all-gather.7.cloned.1.call-done = f32[2048,128]{1,0:T(8,128)} async-done(((f32[64,128]{1,0:T(8,128)}), f32[2048,128]{1,0:T(8,128)}) %all-gather.7.cloned.1.call-update) | async-done | bytes 1048592 | tf_op jit(solution)/shard_map/all_gather | solution.py:61
  261.4 2.7 fusion.5
  264.2 62.7 %all-gather.9.cloned.1.call-done = f32[2048,128]{1,0:T(8,128)} async-done(((f32[64,128]{1,0:T(8,128)}), f32[2048,128]{1,0:T(8,128)}) %all-gather.9.cloned.1.call-update) | async-done | bytes 1048592 | tf_op jit(solution)/shard_map/all_gather | solution.py:73
  327.0 2.1 fusion.3
  329.1 50.6 %all_gather.25 = f32[64,2048]{1,0:T(8,128)S(1)} all-gather(f32[64,128]{1,0:T(8,128)S(1)} %fusion.3), channel_id=1, replica_groups=mesh['dp'=16,'feat'=32] {'dp'}, dimensions={1}, use_global_device_ids=true | all-gather | bytes 557056 | tf_op jit(solution)/shard_map/all_gather | solution.py:77
  379.7 2.1 fusion.4
  381.9 54.6 %all_gather.26 = bf16[2048,128]{1,0:T(8,128)(2,1)} all-gather(bf16[64,128]{1,0:T(8,128)(2,1)S(1)} %fusion.4), channel_id=1, replica_groups=mesh['dp'=16,'feat'=32] {'feat'}, dimensions={0}, use_global_device_ids=true | all-gather | bytes 540672 | tf_op jit(solution)/shard_map/all_gather | solution.py:80
  436.6 220.7 %all-gather.11.cloned.1.call-done = bf16[2048,2048]{1,0:T(8,128)(2,1)} async-done(((bf16[2048,128]{1,0:T(8,128)(2,1)}), bf16[2048,2048]{1,0:T(8,128)(2,1)}) %all-gather.11.cloned.1.call-update) | async-done | bytes 8388624 | tf_op jit(solution)/shard_map/all_gather | solution.py:83
  657.3 5.1 multiply_reduce_fusion.1
  662.3 1.4 gather_fusion
  663.7 1.6 convert_select_fusion
  665.3 107.9 %all-reduce.1 = bf16[256,2048]{1,0:T(8,128)(2,1)S(1)} all-reduce(f32[256,2048]{1,0:T(8,128)} %convert_select_fusion), channel_id=1, replica_groups=mesh['dp'=16,'feat'=32] {'dp','feat'}, use_global_device_ids=true, to_apply=%region_4.5 | all-reduce | flops 524288 | bytes 3145728 | tf_op jit(solution)/shard_map/psum | solution.py:87
  773.2 0.3 multiply_reduce_fusion
  773.4 0.5 fusion.2
  774.0 0.5 multiply_minimum_fusion
  (24 shorter events, 0.3 us)
Async XLA Ops:
  6.5 650.7 %copy-start = (bf16[64,2048]{1,0:T(8,128)(2,1)S(1)}, bf16[64,2048]{1,0:T(8,128)(2,1)}, u32[]{:S(2)}) copy-start(bf16[64,2048]{1,0:T(8,128)(2,1)} %param.5) | copy-start | bytes 786436
  6.5 80.9 %copy-start.1 = (bf16[32,2048]{1,0:T(8,128)(2,1)S(1)}, bf16[32,2048]{1,0:T(8,128)(2,1)}, u32[]{:S(2)}) copy-start(bf16[32,2048]{1,0:T(8,128)(2,1)} %param.4) | copy-start | bytes 393220
  6.5 76.8 %all-gather.5.cloned.1.call-start = ((), (), s32[]{:S(2)}) async-start(), calls=%async_computation.1 | async-start | bytes 4325376 | tf_op jit(solution)/shard_map/all_gather | solution.py:52
  7.3 189.5 %reduce-scatter.2.cloned.1.call-start = ((), (), s32[]{:S(2)}) async-start(), calls=%async_computation.2 | async-start | bytes 557056 | tf_op jit(solution)/shard_map/reduce_scatter | solution.py:58
  87.4 349.2 %copy-start.2 = (s32[256]{0:T(256)S(1)}, s32[256]{0:T(256)}, u32[]{:S(2)}) copy-start(s32[256]{0:T(256)} %param.7) | copy-start | bytes 3076
  87.4 174.0 %all-gather.7.cloned.1.call-start = ((), (), s32[]{:S(2)}) async-start(), calls=%async_computation.3 | async-start | bytes 1081344 | tf_op jit(solution)/shard_map/all_gather | solution.py:61
  198.2 128.8 %all-gather.9.cloned.1.call-start = ((), (), s32[]{:S(2)}) async-start(), calls=%async_computation.4 | async-start | bytes 1081344 | tf_op jit(solution)/shard_map/all_gather | solution.py:73
  264.2 393.1 %all-gather.11.cloned.1.call-start = ((), (), s32[]{:S(2)}) async-start(), calls=%async_computation.5 | async-start | bytes 8912896 | tf_op jit(solution)/shard_map/all_gather | solution.py:83
  663.7 110.3 %copy-start.3 = (f32[64]{0:T(128)S(1)}, f32[64]{0:T(128)}, u32[]{:S(2)}) copy-start(f32[64]{0:T(128)} %param.6) | copy-start | bytes 772
Sparse Core Ops, SparseCore 0:
  9.5 73.7 all-gather.4
  87.5 109.1 reduce-scatter.1
  199.1 62.2 all-gather.6
  264.3 62.6 all-gather.8
  436.6 220.5 all-gather.10
where the time goes:
time: 782 us; the launch traced here: 781 us
  waiting for transfers between devices  375 us (48%)
  blocking collectives  371 us (47%)
  matrix products  16.6 us (2%)
  between operations  13.3 us (2%)
    all_gather x1, waiting for transfers between devices, per_device(): lax.all_gather(weight_cols, 'dp', axis=1, tiled=True)  221 us
    psum x1, blocking collectives, per_device(): centre_full = lax.psum(contribution, ('dp', 'feat')).astype(jnp.bfloat16)  108 us
    psum x1, blocking collectives, per_device(): col_squares = lax.psum(own_squares, ('dp', 'feat'))  105 us
    all_gather x1, waiting for transfers between devices, per_device(): portion = lax.all_gather(sample, 'feat', axis=0, tiled=True)  76 us
    all_gather x1, waiting for transfers between devices, per_device(): lax.all_gather(updated_y, 'feat', axis=0, tiled=True)  62.7 us
    all_gather x1, blocking collectives, per_device(): weight_cols = lax.all_gather(weight_block, 'feat', axis=0, tiled=True)  54.6 us
    all_gather x1, blocking collectives, per_device(): corr_rows = lax.all_gather(corr_block, 'dp', axis=1, tiled=True)  51.9 us
    all_gather x1, blocking collectives, per_device(): lax.all_gather(second_factor, 'dp', axis=1, tiled=True)  50.6 us
  transfers between devices with their start and end apart: 5, of which 5 were waited for; matrix products, arithmetic and copies ran while one was open for 0% of the time, Pallas kernels for 0%

commit v1 on v0

--- a/solution.py
+++ b/solution.py
@@ -47,7 +47,7 @@
     row_offset = (group_index * feat_count + feat_index) * pool_count
     sample_wide = sample.astype(jnp.float32)
     own_squares = jnp.sum(sample_wide * sample_wide, axis=0)
-    col_squares = lax.psum(own_squares, ("dp", "feat"))
+    col_squares = jnp.sum(lax.all_gather(own_squares, ("dp", "feat")), axis=0)
     inverse = 1.0 / jnp.sqrt(col_squares / sample_total + EPSILON)
     portion = lax.all_gather(sample, "feat", axis=0, tiled=True)
     left_part = lax.dynamic_slice_in_dim(portion, row_start, row_block, 1)

time: 782 us -> 1590 us (2.03)
  waiting for transfers between devices: 375 us -> 1280 us
  blocking collectives: 371 us -> 263 us
    all_gather x0 -> x1, waiting for transfers between devices: none -> 803 us  [per_device(): col_squares = jnp.sum(lax.all_gather(own_squares, ('dp', 'feat')), axis=0)]
    psum x1 -> x0, blocking collectives: 105 us -> none  [per_device(): col_squares = lax.psum(own_squares, ('dp', 'feat'))]
    reduce_scatter x1, waiting for transfers between devices: 3.57 us -> 107 us  [per_device(): lax.psum_scatter(gram_part, 'dp', scatter_dimension=1, tiled=True)]
  transfers between devices with their start and end apart: 5 -> 6, of which waited for: 5 -> 6; matrix products, arithmetic and copies ran while one was open for 0% -> 1% of each run, Pallas kernels for 0% -> 0%
where the time goes in v1:
time: 1590 us
  waiting for transfers between devices  1280 us (81%)
  blocking collectives  263 us (17%)
  matrix products  16.7 us (1%)
    all_gather x1, waiting for transfers between devices, per_device(): col_squares = jnp.sum(lax.all_gather(own_squares, ('dp', 'feat')), axis=0)  803 us
    all_gather x1, waiting for transfers between devices, per_device(): lax.all_gather(weight_cols, 'dp', axis=1, tiled=True)  223 us
    psum x1, blocking collectives, per_device(): centre_full = lax.psum(contribution, ('dp', 'feat')).astype(jnp.bfloat16)  108 us
    reduce_scatter x1, waiting for transfers between devices, per_device(): lax.psum_scatter(gram_part, 'dp', scatter_dimension=1, tiled=True)  107 us
    all_gather x1, waiting for transfers between devices, per_device(): portion = lax.all_gather(sample, 'feat', axis=0, tiled=True)  74.4 us
    all_gather x1, waiting for transfers between devices, per_device(): lax.all_gather(updated_y, 'feat', axis=0, tiled=True)  62.5 us
    all_gather x1, blocking collectives, per_device(): weight_cols = lax.all_gather(weight_block, 'feat', axis=0, tiled=True)  52.7 us
    all_gather x1, blocking collectives, per_device(): corr_rows = lax.all_gather(corr_block, 'dp', axis=1, tiled=True)  51.7 us
  transfers between devices with their start and end apart: 6, of which 6 were waited for; matrix products, arithmetic and copies ran while one was open for 1% of the time, Pallas kernels for 0%

profile of v1, /device:TPU:1, one launch (start us, length us, event | category | flops | bytes accessed | tf_op | source)
XLA Modules:
  0.0 1589.4 jit_solution(2997330600667834882)
XLA Ops:
  6.5 0.7 all-gather.7.cloned.1.call-update
  7.3 1.5 multiply_reduce_fusion.2
  8.9 74.4 %all-gather.7.cloned.1.call-done = bf16[1024,2048]{1,0:T(8,128)(2,1)} async-done(((bf16[32,2048]{1,0:T(8,128)(2,1)}), bf16[1024,2048]{1,0:T(8,128)(2,1)}) %all-gather.7.cloned.1.call-update) | async-done | bytes 4194320 | tf_op jit(solution)/shard_map/all_gather | solution.py:52
  83.3 4.1 convolution_multiply_fusion
  87.5 802.9 %all-gather.15.cloned.1.call-done = f32[1048576]{0:T(1024)} async-done(((f32[2048]{0:T(1024)}), f32[1048576]{0:T(1024)}) %all-gather.15.cloned.1.call-update) | async-done | bytes 4194320 | tf_op jit(solution)/shard_map/all_gather | solution.py:50
  890.4 4.9 reshape.21
  895.3 2.4 reduce_sum.37
  897.9 107.3 %reduce-scatter.2.cloned.1.call-done = f32[64,128]{1,0:T(8,128)} async-done(((f32[64,2048]{1,0:T(8,128)}), f32[64,128]{1,0:T(8,128)}) %reduce-scatter.2.cloned.1.call-update) | async-done | bytes 32784 | tf_op jit(solution)/shard_map/reduce_scatter | solution.py:58
  1005.2 1.4 multiply_multiply_fusion
  1006.7 51.7 %all_gather.30 = f32[64,2048]{1,0:T(8,128)S(1)} all-gather(f32[64,128]{1,0:T(8,128)} %multiply_multiply_fusion), channel_id=1, replica_groups=mesh['dp'=16,'feat'=32] {'dp'}, dimensions={1}, use_global_device_ids=true | all-gather | bytes 557056 | tf_op jit(solution)/shard_map/all_gather | solution.py:60
  1058.4 11.0 all-gather.9.cloned.1.call-done
  1069.5 2.7 fusion.5
  1072.3 62.5 %all-gather.11.cloned.1.call-done = f32[2048,128]{1,0:T(8,128)} async-done(((f32[64,128]{1,0:T(8,128)}), f32[2048,128]{1,0:T(8,128)}) %all-gather.11.cloned.1.call-update) | async-done | bytes 1048592 | tf_op jit(solution)/shard_map/all_gather | solution.py:73
  1134.8 2.1 fusion.3
  1136.9 50.9 %all_gather.33 = f32[64,2048]{1,0:T(8,128)S(1)} all-gather(f32[64,128]{1,0:T(8,128)S(1)} %fusion.3), channel_id=1, replica_groups=mesh['dp'=16,'feat'=32] {'dp'}, dimensions={1}, use_global_device_ids=true | all-gather | bytes 557056 | tf_op jit(solution)/shard_map/all_gather | solution.py:77
  1187.8 2.1 fusion.4
  1189.9 52.7 %all_gather.34 = bf16[2048,128]{1,0:T(8,128)(2,1)} all-gather(bf16[64,128]{1,0:T(8,128)(2,1)S(1)} %fusion.4), channel_id=1, replica_groups=mesh['dp'=16,'feat'=32] {'feat'}, dimensions={0}, use_global_device_ids=true | all-gather | bytes 540672 | tf_op jit(solution)/shard_map/all_gather | solution.py:80
  1242.7 222.7 %all-gather.13.cloned.1.call-done = bf16[2048,2048]{1,0:T(8,128)(2,1)} async-done(((bf16[2048,128]{1,0:T(8,128)(2,1)}), bf16[2048,2048]{1,0:T(8,128)(2,1)}) %all-gather.13.cloned.1.call-update) | async-done | bytes 8388624 | tf_op jit(solution)/shard_map/all_gather | solution.py:83
  1465.3 5.1 multiply_reduce_fusion.1
  1470.4 1.4 gather_fusion
  1471.8 1.6 convert_select_fusion
  1473.3 107.9 %all-reduce.1 = bf16[256,2048]{1,0:T(8,128)(2,1)S(1)} all-reduce(f32[256,2048]{1,0:T(8,128)} %convert_select_fusion), channel_id=1, replica_groups=mesh['dp'=16,'feat'=32] {'dp','feat'}, use_global_device_ids=true, to_apply=%region_4.5 | all-reduce | flops 524288 | bytes 3145728 | tf_op jit(solution)/shard_map/psum | solution.py:87
  1581.5 0.5 fusion.2
  1582.0 0.5 multiply_minimum_fusion
  (26 shorter events, 0.8 us)
Async XLA Ops:
  6.5 1458.8 %copy-start = (bf16[64,2048]{1,0:T(8,128)(2,1)S(1)}, bf16[64,2048]{1,0:T(8,128)(2,1)}, u32[]{:S(2)}) copy-start(bf16[64,2048]{1,0:T(8,128)(2,1)} %param.5) | copy-start | bytes 786436
  6.5 76.8 %all-gather.7.cloned.1.call-start = ((), (), s32[]{:S(2)}) async-start(), calls=%async_computation.1 | async-start | bytes 4325376 | tf_op jit(solution)/shard_map/all_gather | solution.py:52
  7.3 883.1 %all-gather.15.cloned.1.call-start = ((), (), s32[]{:S(2)}) async-start(), calls=%async_computation.6 | async-start | bytes 4202496 | tf_op jit(solution)/shard_map/all_gather | solution.py:50
  8.9 996.3 %reduce-scatter.2.cloned.1.call-start = ((), (), s32[]{:S(2)}) async-start(), calls=%async_computation.2 | async-start | bytes 557056 | tf_op jit(solution)/shard_map/reduce_scatter | solution.py:58
  87.4 982.0 %all-gather.9.cloned.1.call-start = ((), (), s32[]{:S(2)}) async-start(), calls=%async_computation.3 | async-start | bytes 1081344 | tf_op jit(solution)/shard_map/all_gather | solution.py:61
  897.7 344.9 %copy-start.1 = (s32[256]{0:T(256)S(1)}, s32[256]{0:T(256)}, u32[]{:S(2)}) copy-start(s32[256]{0:T(256)} %param.7) | copy-start | bytes 3076
  1006.6 128.2 %all-gather.11.cloned.1.call-start = ((), (), s32[]{:S(2)}) async-start(), calls=%async_computation.4 | async-start | bytes 1081344 | tf_op jit(solution)/shard_map/all_gather | solution.py:73
  1072.2 393.1 %all-gather.13.cloned.1.call-start = ((), (), s32[]{:S(2)}) async-start(), calls=%async_computation.5 | async-start | bytes 8912896 | tf_op jit(solution)/shard_map/all_gather | solution.py:83
  1471.8 110.3 %copy-start.2 = (f32[64]{0:T(128)S(1)}, f32[64]{0:T(128)}, u32[]{:S(2)}) copy-start(f32[64]{0:T(128)} %param.6) | copy-start | bytes 772
Sparse Core Ops, SparseCore 0:
  9.5 73.7 all-gather.6
  85.5 804.7 all-gather.14
  894.4 110.6 reduce-scatter.1
  1007.4 62.0 all-gather.8
  1072.4 62.4 all-gather.10
  1242.7 222.5 all-gather.12

commit v2 on v0

--- a/solution.py
+++ b/solution.py
@@ -70,7 +70,11 @@
     updated_y = jnp.dot(corr_rows, first_cols, precision=HIGHEST)
     left_part = first_rows
     middle = jnp.dot(
-        left_part, lax.all_gather(updated_y, "feat", axis=0, tiled=True), precision=HIGHEST
+        left_part,
+        jnp.concatenate(
+            lax.all_to_all(jnp.stack([updated_y] * lax.axis_size("feat")), "feat", 0, 0), axis=0
+        ),
+        precision=HIGHEST,
     )
     second_factor = 0.5 * (3.0 * eye_block - middle)
     root_block = jnp.dot(

time: 782 us -> 748 us (0.957)
  waiting for transfers between devices: 375 us -> 342 us
    all_gather x1 -> x0, waiting for transfers between devices: 62.7 us -> none  [per_device(): lax.all_gather(updated_y, 'feat', axis=0, tiled=True)]
    all_to_all x0 -> x1, waiting for transfers between devices: none -> 27.8 us  [per_device(): lax.all_to_all(jnp.stack([updated_y] * lax.axis_size('feat')), 'feat', 0, 0)]
where the time goes in v2:
time: 748 us
  blocking collectives  366 us (49%)
  waiting for transfers between devices  342 us (46%)
  matrix products  13.7 us (2%)
  between operations  13.3 us (2%)
    all_gather x1, waiting for transfers between devices, per_device(): lax.all_gather(weight_cols, 'dp', axis=1, tiled=True)  223 us
    psum x1, blocking collectives, per_device(): centre_full = lax.psum(contribution, ('dp', 'feat')).astype(jnp.bfloat16)  108 us
    psum x1, blocking collectives, per_device(): col_squares = lax.psum(own_squares, ('dp', 'feat'))  106 us
    all_gather x1, waiting for transfers between devices, per_device(): portion = lax.all_gather(sample, 'feat', axis=0, tiled=True)  76 us
    all_gather x1, blocking collectives, per_device(): corr_rows = lax.all_gather(corr_block, 'dp', axis=1, tiled=True)  51.8 us
    all_gather x1, blocking collectives, per_device(): lax.all_gather(second_factor, 'dp', axis=1, tiled=True)  50.1 us
    all_gather x1, blocking collectives, per_device(): weight_cols = lax.all_gather(weight_block, 'feat', axis=0, tiled=True)  50.1 us
    all_to_all x1, waiting for transfers between devices, per_device(): lax.all_to_all(jnp.stack([updated_y] * lax.axis_size('feat')), 'feat', 0, 0)  27.8 us
  transfers between devices with their start and end apart: 5, of which 5 were waited for; matrix products, arithmetic and copies ran while one was open for 0% of the time, Pallas kernels for 0%

profile of v2, /device:TPU:1, one launch (start us, length us, event | category | flops | bytes accessed | tf_op | source)
XLA Modules:
  0.0 747.7 jit_solution(14212397018333000163)
XLA Ops:
  6.5 0.7 all-gather.4.cloned.1.call-update
  7.3 76.0 %all-gather.4.cloned.1.call-done = bf16[1024,2048]{1,0:T(8,128)(2,1)} async-done(((bf16[32,2048]{1,0:T(8,128)(2,1)}), bf16[1024,2048]{1,0:T(8,128)(2,1)}) %all-gather.4.cloned.1.call-update) | async-done | bytes 4194320 | tf_op jit(solution)/shard_map/all_gather | solution.py:52
  83.3 4.0 convolution_multiply_fusion
  87.5 105.6 %psum.14 = f32[2048]{0:T(1024)S(1)} all-reduce(f32[2048]{0:T(1024)S(1)} %multiply_reduce_fusion.2), channel_id=1, replica_groups=mesh['dp'=16,'feat'=32] {'dp','feat'}, use_global_device_ids=true, to_apply=%region_1.0 | all-reduce | flops 2048 | bytes 16384 | tf_op jit(solution)/shard_map/psum | solution.py:50
  193.2 3.4 reduce-scatter.2.cloned.1.call-done
  196.6 1.4 multiply_multiply_fusion
  198.1 51.8 %all_gather.19 = f32[64,2048]{1,0:T(8,128)S(1)} all-gather(f32[64,128]{1,0:T(8,128)} %multiply_multiply_fusion), channel_id=1, replica_groups=mesh['dp'=16,'feat'=32] {'dp'}, dimensions={1}, use_global_device_ids=true | all-gather | bytes 557056 | tf_op jit(solution)/shard_map/all_gather | solution.py:60
  249.9 11.3 %all-gather.6.cloned.1.call-done = f32[2048,128]{1,0:T(8,128)} async-done(((f32[64,128]{1,0:T(8,128)}), f32[2048,128]{1,0:T(8,128)}) %all-gather.6.cloned.1.call-update) | async-done | bytes 1048592 | tf_op jit(solution)/shard_map/all_gather | solution.py:61
  261.2 2.2 fusion.5
  263.4 1.2 stack.2
  264.6 6.3 all-to-all-start
  271.0 27.8 %all-to-all-done = f32[32,64,128]{2,1,0:T(8,128)S(1)} async-done(((f32[32,64,128]{2,1,0:T(8,128)}), f32[32,64,128]{2,1,0:T(8,128)S(1)}, u32[]{:S(2)}, u32[]{:S(2)}) %all-to-all-start) | async-done | bytes 1048608 | tf_op jit(solution)/shard_map/all_to_all | solution.py:75
  298.8 0.9 fusion.3
  299.7 50.1 %all_gather.21 = f32[64,2048]{1,0:T(8,128)S(1)} all-gather(f32[64,128]{1,0:T(8,128)S(1)} %fusion.3), channel_id=1, replica_groups=mesh['dp'=16,'feat'=32] {'dp'}, dimensions={1}, use_global_device_ids=true | all-gather | bytes 557056 | tf_op jit(solution)/shard_map/all_gather | solution.py:81
  349.8 0.9 fusion.4
  350.7 50.1 %all_gather.22 = bf16[2048,128]{1,0:T(8,128)(2,1)} all-gather(bf16[64,128]{1,0:T(8,128)(2,1)S(1)} %fusion.4), channel_id=1, replica_groups=mesh['dp'=16,'feat'=32] {'feat'}, dimensions={0}, use_global_device_ids=true | all-gather | bytes 540672 | tf_op jit(solution)/shard_map/all_gather | solution.py:84
  400.9 222.9 %all-gather.8.cloned.1.call-done = bf16[2048,2048]{1,0:T(8,128)(2,1)} async-done(((bf16[2048,128]{1,0:T(8,128)(2,1)}), bf16[2048,2048]{1,0:T(8,128)(2,1)}) %all-gather.8.cloned.1.call-update) | async-done | bytes 8388624 | tf_op jit(solution)/shard_map/all_gather | solution.py:87
  623.9 5.1 multiply_reduce_fusion.1
  628.9 1.4 gather_fusion
  630.3 1.6 convert_select_fusion
  631.9 107.9 %all-reduce.1 = bf16[256,2048]{1,0:T(8,128)(2,1)S(1)} all-reduce(f32[256,2048]{1,0:T(8,128)} %convert_select_fusion), channel_id=1, replica_groups=mesh['dp'=16,'feat'=32] {'dp','feat'}, use_global_device_ids=true, to_apply=%region_4.5 | all-reduce | flops 524288 | bytes 3145728 | tf_op jit(solution)/shard_map/psum | solution.py:91
  739.8 0.3 multiply_reduce_fusion
  740.1 0.5 fusion.2
  740.6 0.5 multiply_minimum_fusion
  (26 shorter events, 0.4 us)
Async XLA Ops:
  6.5 617.3 %copy-start = (bf16[64,2048]{1,0:T(8,128)(2,1)S(1)}, bf16[64,2048]{1,0:T(8,128)(2,1)}, u32[]{:S(2)}) copy-start(bf16[64,2048]{1,0:T(8,128)(2,1)} %param.5) | copy-start | bytes 786436
  6.5 80.9 %copy-start.2 = (bf16[32,2048]{1,0:T(8,128)(2,1)S(1)}, bf16[32,2048]{1,0:T(8,128)(2,1)}, u32[]{:S(2)}) copy-start(bf16[32,2048]{1,0:T(8,128)(2,1)} %param.4) | copy-start | bytes 393220
  6.5 76.8 %all-gather.4.cloned.1.call-start = ((), (), s32[]{:S(2)}) async-start(), calls=%async_computation.2 | async-start | bytes 4325376 | tf_op jit(solution)/shard_map/all_gather | solution.py:52
  7.3 189.4 %reduce-scatter.2.cloned.1.call-start = ((), (), s32[]{:S(2)}) async-start(), calls=%async_computation.3 | async-start | bytes 557056 | tf_op jit(solution)/shard_map/reduce_scatter | solution.py:58
  87.4 173.8 %all-gather.6.cloned.1.call-start = ((), (), s32[]{:S(2)}) async-start(), calls=%async_computation.4 | async-start | bytes 1081344 | tf_op jit(solution)/shard_map/all_gather | solution.py:61
  261.2 88.6 %copy-start.1 = (f32[2048,128]{1,0:T(8,128)S(1)}, f32[2048,128]{1,0:T(8,128)}, u32[]{:S(2)}) copy-start(f32[2048,128]{1,0:T(8,128)} %all-gather.6.cloned.1.call-done) | copy-start | bytes 3145732
  263.4 137.4 %copy-start.3 = (s32[256]{0:T(256)S(1)}, s32[256]{0:T(256)}, u32[]{:S(2)}) copy-start(s32[256]{0:T(256)} %param.7) | copy-start | bytes 3076
  264.6 34.2 %all-to-all-start = ((f32[32,64,128]{2,1,0:T(8,128)}), f32[32,64,128]{2,1,0:T(8,128)S(1)}, u32[]{:S(2)}, u32[]{:S(2)}) async-start(f32[32,64,128]{2,1,0:T(8,128)} %stack.2), calls=%async_computation.1 | async-start | bytes 2097152 | tf_op jit(solution)/shard_map/all_to_all | solution.py:75
  270.9 353.0 %all-gather.8.cloned.1.call-start = ((), (), s32[]{:S(2)}) async-start(), calls=%async_computation.5 | async-start | bytes 8912896 | tf_op jit(solution)/shard_map/all_gather | solution.py:87
  630.3 110.3 %copy-start.4 = (f32[64]{0:T(128)S(1)}, f32[64]{0:T(128)}, u32[]{:S(2)}) copy-start(f32[64]{0:T(128)} %param.6) | copy-start | bytes 772
Sparse Core Ops, SparseCore 0:
  9.5 73.7 all-gather.3
  87.5 109.0 reduce-scatter.1
  199.0 62.1 all-gather.5
  401.0 222.8 all-gather.7
